TPU v7x, 32 devices: a whole 2x2x4 slice. The times are simulated.
32 devices in a mesh: dom: 16 (over z, x, core), orb: 2 (over y).
Axes of the slice: x: 2, y: 2, z: 4, core: 2. Of those that a mesh axis runs over, the one named last changes fastest.
Arguments:
- orbitals: bfloat16 [4, 256, 256, 128], P('orb', 'dom'), may hold values from -2.390625 to 2.390625
- energies: float32 [4], P('orb'), may hold values from -1.5 to -0.3
- local_potential: float32 [256, 256, 128], P('dom'), may hold values from -4 to 4
- lanczos: bfloat16 [4, 256, 256, 128], P('orb', 'dom'), may hold values from -40 to 40
- previous: bfloat16 [4, 256, 256, 128], P('orb', 'dom'), may hold values from -6 to 6
- beta: float32 [1], replicated, may hold values from 0.3 to 1.5
Outputs:
- next_vector: bfloat16 [4, 256, 256, 128], P('orb', 'dom')
- alpha: float32 [1], replicated
- beta_next: float32 [1], replicated
All inputs are finite; a program needn't handle non-finite values.
Results may differ from a plain program's by a relative error of at most 0.0085.
Values may be sent and summed in bfloat16 or wider, within the bound.
No kernel may reach another device: no remote copies, remote signals or barrier semaphores. Data moves between devices by JAX's collectives and lax.ppermute only.
A program may use at most 192 MiB of HBM per device.

v0:
```python
import functools

import jax
import jax.numpy as jnp
import numpy as np
from jax import lax
from jax.experimental import pallas as pl
from jax.experimental.pallas import tpu as pltpu
from jax.sharding import PartitionSpec as P

side_weights = (1.5, -0.15, 1.0 / 90.0)
central_weight = -49.0 / 18.0
screening = 1.0 / 64.0
reach_max = len(side_weights)


def cas_matrix(length):
    position = np.arange(length)
    angle = 2.0 * np.pi / length * ((position[:, None] * position[None, :]) % length)
    return np.cos(angle) + np.sin(angle)


def band_matrix(length, center):
    matrix = center * np.eye(length)
    for offset, weight in enumerate(side_weights):
        for step in (offset + 1, -offset - 1):
            matrix += weight * np.roll(np.eye(length), step, axis=1)
    return matrix


def two_parts(matrix):
    high = matrix.astype(jnp.bfloat16)
    low = (matrix - high.astype(np.float64)).astype(jnp.bfloat16)
    return jnp.asarray(high), jnp.asarray(low)


def wave_square(position, length):
    folded = jnp.minimum(position, length - position).astype(jnp.float32)
    wavenumber = 2.0 * jnp.pi / length * folded
    return wavenumber * wavenumber


def product(spec, table, values):
    values = values.astype(jnp.bfloat16)
    parts = two_parts(table)
    return sum(jnp.einsum(spec, part, values, preferred_element_type=jnp.float32) for part in parts)


def shifted(array, axis, step):
    size = lax.axis_size(axis)
    return lax.ppermute(array, axis, [(i, (i + step) % size) for i in range(size)])


def stencil_body(
    energies,
    beta,
    before,
    current,
    after,
    orbitals,
    previous,
    local_potential,
    band_y,
    band_y_low,
    band_z,
    band_z_low,
    fixed,
    cross,
    weight,
    sums,
    extended,
):
    plane = pl.program_id(0)
    fields, planes, length_y, length_z = current.shape
    half = [-0.5 * w for w in side_weights]
    rows = 64

    @pl.when(plane == 0)
    def _():
        extended[:, :reach_max] = before[...]
        extended[:, reach_max : reach_max + planes] = current[...]
        extended[:, reach_max + planes :] = after[...]
        sums[...] = jnp.zeros_like(sums)

    here = plane + reach_max
    beta_now = beta[0]

    def folded(values):
        return jnp.sum(values.reshape(rows // 8, 8, length_z), axis=0)

    totals = [jnp.zeros((8, length_z), jnp.float32) for _ in range(4)]
    for start in range(0, length_y, rows):
        piece = pl.ds(start, rows)
        local = local_potential[0, piece, :]
        cross_now = jnp.zeros((rows, length_z), jnp.float32)
        weight_now = jnp.zeros((rows, length_z), jnp.float32)
        for i in range(fields):
            whole = extended[i, here]
            narrow = extended[i, here, piece, :]
            dot = functools.partial(jnp.dot, preferred_element_type=jnp.float32)
            value = dot(band_y[piece, :], whole) + dot(band_y_low[piece, :], whole)
            value = value + dot(narrow, band_z[...]) + dot(narrow, band_z_low[...])
            for offset in range(reach_max):
                right = extended[i, here + offset + 1, piece, :].astype(jnp.float32)
                left = extended[i, here - offset - 1, piece, :].astype(jnp.float32)
                value = value + half[offset] * (right + left)
            centre = narrow.astype(jnp.float32)
            value = value + (local - energies[i]) * centre
            older = previous[i, 0, piece, :].astype(jnp.float32)
            orbital = orbitals[i, 0, piece, :].astype(jnp.float32)
            rest = value - beta_now * older
            fixed[i, 0, piece, :] = rest
            cross_now = cross_now + orbital * rest
            weight_now = weight_now + orbital * orbital
            for j, term in enumerate((centre * value, centre * rest, rest * rest, centre * centre)):
                totals[j] = totals[j] + folded(term)
        cross[0, piece, :] = cross_now.astype(cross.dtype)
        weight[0, piece, :] = weight_now.astype(weight.dtype)
    for j in range(4):
        sums[j] += totals[j]


def stencil(energies, beta, before, current, after, orbitals, previous, local_potential):
    fields, planes, length_y, length_z = current.shape
    tables = two_parts(-0.5 * band_matrix(length_y, 3.0 * central_weight))
    tables = tables + two_parts(-0.5 * band_matrix(length_z, 0.0))
    smem = pl.BlockSpec(memory_space=pltpu.SMEM)

    def resident(array):
        return pl.BlockSpec(array.shape, lambda a, n=array.ndim: (0,) * n)

    field_spec = pl.BlockSpec((fields, 1, length_y, length_z), lambda a: (0, a, 0, 0))
    plane_spec = pl.BlockSpec((1, length_y, length_z), lambda a: (a, 0, 0))
    points = planes * length_y * length_z
    return pl.pallas_call(
        stencil_body,
        grid=(planes,),
        in_specs=[smem, smem, resident(before), resident(current), resident(after)]
        + [field_spec, field_spec, plane_spec]
        + [resident(table) for table in tables],
        out_specs=[
            field_spec,
            plane_spec,
            plane_spec,
            pl.BlockSpec((4, 8, length_z), lambda a: (0, 0, 0)),
        ],
        out_shape=[
            jax.ShapeDtypeStruct(current.shape, jnp.float32),
            jax.ShapeDtypeStruct((planes, length_y, length_z), jnp.bfloat16),
            jax.ShapeDtypeStruct((planes, length_y, length_z), jnp.bfloat16),
            jax.ShapeDtypeStruct((4, 8, length_z), jnp.float32),
        ],
        scratch_shapes=[
            pltpu.VMEM((fields, planes + 2 * reach_max, length_y, length_z), current.dtype)
        ],
        compiler_params=pltpu.CompilerParams(dimension_semantics=("arbitrary",)),
        cost_estimate=pl.CostEstimate(
            flops=points * fields * 2 * 2 * (length_y + length_z),
            bytes_accessed=points * (fields * 10 + 8),
            transcendentals=0,
        ),
        name="stencil",
    )(energies, beta, before, current, after, orbitals, previous, local_potential, *tables)


def split_step(orbitals, energies, local_potential, lanczos, previous, beta):
    fields, planes, length_y, length_z = lanczos.shape
    groups = lax.axis_size("orb")
    domains = lax.axis_size("dom")
    devices = groups * domains
    length_x = planes * domains
    own = planes // groups
    modes_y = length_y // devices
    me = lax.axis_index("orb")
    both = ("dom", "orb")

    def part(array, index, dim):
        return lax.dynamic_slice_in_dim(array, index * own, own, axis=dim)

    def density_of(index):
        first = part(orbitals, index, 1).astype(jnp.float32)
        return jnp.sum(first * part(lanczos, index, 1).astype(jnp.float32), axis=0)

    def gathered_sum(local_of, mine):
        total = mine
        for step in range(1, groups):
            sent = local_of((me + step) % groups).astype(jnp.bfloat16)
            total = total + shifted(sent, "orb", step).astype(jnp.float32)
        return total

    density = gathered_sum(density_of, density_of(me))
    before = shifted(lanczos[:, planes - reach_max :], "dom", 1)
    after = shifted(lanczos[:, :reach_max], "dom", -1)

    table_x, table_y, table_z = (cas_matrix(n) for n in (length_x, length_y, length_z))
    spectrum = product("cz,ayz->ayc", table_z, density)
    spectrum = product("by,ayc->abc", table_y, spectrum).astype(jnp.bfloat16)
    spectrum = spectrum.reshape(own, devices, modes_y, length_z).transpose(1, 0, 2, 3)
    spectrum = lax.all_to_all(spectrum, both, split_axis=0, concat_axis=0, tiled=True)
    spectrum = spectrum.reshape(length_x, modes_y, length_z)

    fixed, cross, weight, sums = stencil(
        energies, beta, before, lanczos, after, orbitals, previous, local_potential
    )

    def planes_sum(array):
        return gathered_sum(lambda i: part(array, i, 0), part(array, me, 0).astype(jnp.float32))

    weight = planes_sum(weight)
    cross = planes_sum(cross)

    square_x = wave_square(jnp.arange(length_x, dtype=jnp.int32), length_x)
    index = lax.axis_index("dom") * groups + me
    index_y = index * modes_y + jnp.arange(modes_y, dtype=jnp.int32)
    square_y = wave_square(index_y, length_y)
    square_z = wave_square(jnp.arange(length_z, dtype=jnp.int32), length_z)
    summed = square_x[:, None, None] + square_y[None, :, None] + square_z[None, None, :] + screening
    normalizer = 4.0 * jnp.pi / (length_x * length_y * length_z)
    spectrum = product("ax,xbc->abc", table_x, spectrum) * (normalizer / summed)
    spectrum = product("ax,xbc->abc", table_x, spectrum).astype(jnp.bfloat16)
    spectrum = spectrum.reshape(devices, own, modes_y, length_z)
    spectrum = lax.all_to_all(spectrum, both, split_axis=0, concat_axis=0, tiled=True)
    spectrum = spectrum.transpose(1, 0, 2, 3).reshape(own, length_y, length_z)
    spectrum = product("by,ayz->abz", table_y, spectrum)
    potential = product("cz,abz->abc", table_z, spectrum)

    def lanes(values):
        return jnp.sum(values.reshape(-1, 8, length_z), axis=0)

    late = [lanes(density * potential), lanes(cross * potential), lanes(weight * potential * potential)]
    partial = jnp.concatenate([sums, jnp.stack(late)], axis=0)
    partial = jnp.sum(partial, axis=1)
    partial = jnp.concatenate([partial, jnp.zeros((1, length_z), jnp.float32)], axis=0)
    partial = jnp.broadcast_to(partial[None], (devices,) + partial.shape)
    partial = lax.all_to_all(partial, both, split_axis=0, concat_axis=0, tiled=True)
    moments = jnp.sum(partial, axis=(0, 2))

    narrow = potential.astype(jnp.bfloat16)
    whole = jnp.zeros((planes, length_y, length_z), jnp.bfloat16)
    whole = lax.dynamic_update_slice_in_dim(whole, narrow, me * own, 0)
    for step in range(1, groups):
        source = (me - step) % groups
        whole = lax.dynamic_update_slice_in_dim(whole, shifted(narrow, "orb", step), source * own, 0)
    image = fixed + orbitals.astype(jnp.float32) * whole.astype(jnp.float32)[None]

    entries = float(fields * groups * length_x * length_y * length_z)
    value_mean, rest_mean, square_mean, self_mean, density_mean, cross_mean, weight_mean = (
        moments[j] / entries for j in range(7)
    )
    rayleigh = value_mean + density_mean
    squares = square_mean + 2.0 * cross_mean + weight_mean
    squares = squares - 2.0 * rayleigh * (rest_mean + density_mean) + rayleigh * rayleigh * self_mean
    norm_next = jnp.sqrt(squares + 1e-06)
    remainder = image - rayleigh * lanczos.astype(jnp.float32)
    next_vector = (remainder / norm_next).astype(jnp.bfloat16)
    return (next_vector, jnp.reshape(rayleigh, (1,)), jnp.reshape(norm_next, (1,)))


def extended(array, sides, width):
    for axis, dim in sides:
        size, length = (lax.axis_size(axis), array.shape[dim])
        up = [(i, (i + 1) % size) for i in range(size)]
        down = [(j, i) for i, j in up]
        last = lax.slice_in_dim(array, length - width, length, axis=dim)
        first = lax.slice_in_dim(array, 0, width, axis=dim)
        before = lax.ppermute(last, axis, up)
        after = lax.ppermute(first, axis, down)
        array = jnp.concatenate([before, array, after], axis=dim)
    return array


def cas_table(length):
    position = jnp.arange(length, dtype=jnp.int32)
    phase = position[:, None] * position[None, :] % length
    angle = 2.0 * jnp.pi / length * phase.astype(jnp.float32)
    return jnp.cos(angle) + jnp.sin(angle)


def transform_lateral(values):
    highest = lax.Precision.HIGHEST
    result = jnp.einsum("by,ayz->abz", cas_table(values.shape[1]), values, precision=highest)
    return jnp.einsum("cz,abz->abc", cas_table(values.shape[2]), result, precision=highest)


def plain_step(orbitals, energies, local_potential, lanczos, previous, beta):
    highest = lax.Precision.HIGHEST
    planes = lanczos.shape[1]
    length_y = lanczos.shape[2]
    length_z = lanczos.shape[3]
    length_x = planes * lax.axis_size("dom")
    normalizer = 4.0 * jnp.pi / (length_x * length_y * length_z)
    padded = extended(lanczos, (("dom", 1),), 3).astype(jnp.float32)
    current = padded[:, 3 : 3 + planes]
    laplace = 3.0 * central_weight * current
    for offset, weight in enumerate(side_weights):
        reach = offset + 1
        laplace = laplace + weight * (
            padded[:, 3 + reach : 3 + reach + planes] + padded[:, 3 - reach : 3 - reach + planes]
        )
        for dimension in (2, 3):
            laplace = laplace + weight * (
                jnp.roll(current, reach, dimension) + jnp.roll(current, -reach, dimension)
            )
    partial_density = jnp.sum(orbitals.astype(jnp.float32) * current, axis=0)
    square_x = wave_square(jnp.arange(length_x, dtype=jnp.int32), length_x)
    table_x = cas_table(length_x)
    density = lax.psum(partial_density.astype(jnp.bfloat16), "orb").astype(jnp.float32)
    spectrum = lax.all_to_all(
        transform_lateral(density), "dom", split_axis=1, concat_axis=0, tiled=True
    )
    row_count = spectrum.shape[1]
    index_y = lax.axis_index("dom") * row_count + jnp.arange(row_count, dtype=jnp.int32)
    square_y = wave_square(index_y, length_y)
    square_z = wave_square(jnp.arange(length_z, dtype=jnp.int32), length_z)
    summed = square_x[:, None, None] + square_y[None, :, None] + square_z[None, None, :] + screening
    spectrum = jnp.einsum("ax,xbc->abc", table_x, spectrum, precision=highest) * (
        normalizer / summed
    )
    spectrum = jnp.einsum("ax,xbc->abc", table_x, spectrum, precision=highest)
    spectrum = lax.all_to_all(
        spectrum.astype(jnp.bfloat16), "dom", split_axis=0, concat_axis=1, tiled=True
    ).astype(spectrum.dtype)
    potential = transform_lateral(spectrum)
    image = -0.5 * laplace + (local_potential[None] - energies[:, None, None, None]) * current
    image = image + orbitals.astype(jnp.float32) * potential[None]
    entries = float(lanczos.shape[0] * lax.axis_size("orb") * length_x * length_y * length_z)
    older = previous.astype(jnp.float32)
    beta_now = beta[0]
    moments = lax.psum(
        (
            jnp.sum(current * image),
            jnp.sum(image * image),
            jnp.sum(older * image),
            jnp.sum(current * current),
            jnp.sum(current * older),
            jnp.sum(older * older),
        ),
        ("dom", "orb"),
    )
    cross_mean = moments[0] / entries
    image_mean = moments[1] / entries
    older_image = moments[2] / entries
    self_mean = moments[3] / entries
    mixed_mean = moments[4] / entries
    older_mean = moments[5] / entries
    squares = image_mean - 2.0 * cross_mean * cross_mean - 2.0 * beta_now * older_image
    squares = (
        squares + cross_mean * cross_mean * self_mean + 2.0 * cross_mean * beta_now * mixed_mean
    )
    squares = squares + beta_now * beta_now * older_mean
    remainder = image - cross_mean * current - beta_now * older
    norm_next = jnp.sqrt(squares + 1e-06)
    next_vector = (remainder / norm_next).astype(jnp.bfloat16)
    return (next_vector, jnp.reshape(cross_mean, (1,)), jnp.reshape(norm_next, (1,)))


def per_device(orbitals, energies, local_potential, lanczos, previous, beta):
    fields, planes, length_y, length_z = lanczos.shape
    groups = lax.axis_size("orb")
    devices = groups * lax.axis_size("dom")
    fits = planes % groups == 0 and planes >= reach_max
    fits = fits and length_y % (8 * devices) == 0 and length_z % 128 == 0
    step = split_step if fits else plain_step
    return step(orbitals, energies, local_potential, lanczos, previous, beta)


def solution(mesh):
    return jax.shard_map(
        per_device,
        mesh=mesh,
        in_specs=(
            P("orb", "dom", None, None),
            P("orb"),
            P("dom", None, None),
            P("orb", "dom", None, None),
            P("orb", "dom", None, None),
            P(),
        ),
        out_specs=(P("orb", "dom", None, None), P(), P()),
        check_vma=False,
    )
```

profile of v0, /device:TPU:0, one launch (start us, length us, event | category | flops | bytes accessed | tf_op | source)
XLA Modules:
  0.0 146.5 jit_solution(9908144531771165604)
XLA Ops:
  0.7 3.0 %multiply_reduce_fusion = (bf16[8,256,128]{2,1,0:T(8,128)(2,1)S(1)}, f32[8,256,128]{2,1,0:T(8,128)S(1)}) fusion(bf16[2,16,256,128]{3,2,1,0:T(8,128)(2,1)} %current.1, s32[]{:T(128)S(6)} %select_n.33, bf16[2,16,256,128]{3,2,1,0:T(8,128)(2,1)} %orbitals.1, s32[]{:T(128)S(6)} %select_n.31), kind=kLoop, calls=%fused_computation.1 | loop fusion | flops 3670016 | bytes 5767176 | tf_op jit(solution)/shard_map/reduce_sum | solution.py:182
  3.7 3.1 %collective-permute-start.2 = (bf16[8,256,128]{2,1,0:T(8,128)(2,1)S(1)}, bf16[8,256,128]{2,1,0:T(8,128)(2,1)S(1)}, u32[]{:S(2)}, u32[]{:S(2)}) collective-permute-start(bf16[8,256,128]{2,1,0:T(8,128)(2,1)S(1)} %get-tuple-element.11), channel_id=1, source_target_pairs={{0,1},{1,0},{2,3},{3,2},{4,5},{5,4},{6,7},{7,6},{8,9},{9,8},{10,11... | collective-permute-start | bytes 1572872 | tf_op jit(solution)/shard_map/ppermute | solution.py:51
  6.8 11.9 %collective-permute-done.2 = bf16[8,256,128]{2,1,0:T(8,128)(2,1)S(1)} collective-permute-done((bf16[8,256,128]{2,1,0:T(8,128)(2,1)S(1)}, bf16[8,256,128]{2,1,0:T(8,128)(2,1)S(1)}, u32[]{:S(2)}, u32[]{:S(2)}) %collective-permute-start.2) | collective-permute-done | bytes 524320 | tf_op jit(solution)/shard_map/ppermute | solution.py:51
  21.9 6.1 %all-to-all-start = ((bf16[32,8,8,128]{3,2,1,0:T(8,128)(2,1)}), bf16[32,8,8,128]{3,2,1,0:T(8,128)(2,1)S(1)}, u32[]{:S(2)}, u32[]{:S(2)}) async-start(bf16[32,8,8,128]{3,2,1,0:T(8,128)(2,1)} %copy.58), calls=%async_computation | async-start | bytes 1048576 | tf_op jit(solution)/shard_map/all_to_all | solution.py:199
  28.1 14.8 %all-to-all-done = bf16[32,8,8,128]{3,2,1,0:T(8,128)(2,1)S(1)} async-done(((bf16[32,8,8,128]{3,2,1,0:T(8,128)(2,1)}), bf16[32,8,8,128]{3,2,1,0:T(8,128)(2,1)S(1)}, u32[]{:S(2)}, u32[]{:S(2)}) %all-to-all-start) | async-done | bytes 524320 | tf_op jit(solution)/shard_map/all_to_all | solution.py:199
  45.7 3.6 %all-to-all-start.1 = ((bf16[32,8,8,128]{3,2,1,0:T(8,128)(2,1)}), bf16[32,8,8,128]{3,2,1,0:T(8,128)(2,1)S(1)}, u32[]{:S(2)}, u32[]{:S(2)}) async-start(bf16[32,8,8,128]{3,2,1,0:T(8,128)(2,1)} %bitcast.10), calls=%async_computation.1 | async-start | bytes 1048576 | tf_op jit(solution)/shard_map/all_to_all | solution.py:222
  49.3 1.2 fusion.29
  50.8 4.2 %collective-permute-start.1 = (bf16[2,3,256,128]{3,2,1,0:T(8,128)(2,1)S(1)}, bf16[2,3,256,128]{3,2,1,0:T(8,128)(2,1)S(1)}, u32[]{:S(2)}, u32[]{:S(2)}) collective-permute-start(bf16[2,3,256,128]{3,2,1,0:T(8,128)(2,1)S(1)} %get-tuple-element.15), channel_id=1, source_target_pairs={{0,30},{2,0},{4,2},{6,4},{8,6},{10,8},{12,10},{14,12},{16,14},{18,... | collective-permute-start | bytes 1179656 | tf_op jit(solution)/shard_map/ppermute | solution.py:51
  55.7 11.9 %collective-permute-done.before = bf16[2,3,256,128]{3,2,1,0:T(8,128)(2,1)S(1)} collective-permute-done((bf16[2,3,256,128]{3,2,1,0:T(8,128)(2,1)S(1)}, bf16[2,3,256,128]{3,2,1,0:T(8,128)(2,1)S(1)}, u32[]{:S(2)}, u32[]{:S(2)}) %collective-permute-start) | collective-permute-done | bytes 393248 | tf_op jit(solution)/shard_map/ppermute | solution.py:51
  69.1 15.9 %stencil.1 = (f32[2,16,256,128]{3,2,1,0:T(8,128)}, bf16[16,256,128]{2,1,0:T(8,128)(2,1)}, bf16[16,256,128]{2,1,0:T(8,128)(2,1)}, f32[4,8,128]{2,1,0:T(8,128)}) custom-call(f32[2]{0:T(128)} %energies.1, f32[1]{0:T(128)S(6)} %copy.83.beta, bf16[2,3,256,128]{3,2,1,0:T(8,128)(2,1)} %copy-done.8, bf16[2,16,256,128]{3,2,1,0:T(8,128)(2,1)} %current.1, ...), custom_call_target="tpu_custom_call" | custom-call | flops 1610612736 | bytes 14680064 | tf_op jit(solution)/shard_map/stencil/pallas_call | solution.py:135
  85.0 1.9 %constant_dynamic-slice_fusion.1 = bf16[8,256,128]{2,1,0:T(8,128)(2,1)} fusion(bf16[16,256,128]{2,1,0:T(8,128)(2,1)} %get-tuple-element.10, s32[]{:T(128)S(6)} %select_n.33), kind=kLoop, calls=%fused_computation.34 | loop fusion | bytes 1048580 | tf_op jit(solution)/shard_map/dynamic_slice | solution.py:178
  87.0 1.5 %collective-permute-start.5 = (bf16[8,256,128]{2,1,0:T(8,128)(2,1)}, bf16[8,256,128]{2,1,0:T(8,128)(2,1)S(1)}, u32[]{:S(2)}, u32[]{:S(2)}) collective-permute-start(bf16[8,256,128]{2,1,0:T(8,128)(2,1)} %constant_dynamic-slice_fusion.1), channel_id=1, source_target_pairs={{0,1},{1,0},{2,3},{3,2},{4,5},{5,4},{6,7},{7,6},{8,9},{9,8},{10,11... | collective-permute-start | bytes 1572872 | tf_op jit(solution)/shard_map/ppermute | solution.py:51
  88.5 1.9 %constant_dynamic-slice_fusion = bf16[8,256,128]{2,1,0:T(8,128)(2,1)} fusion(bf16[16,256,128]{2,1,0:T(8,128)(2,1)} %get-tuple-element.9, s32[]{:T(128)S(6)} %select_n.33), kind=kLoop, calls=%fused_computation.31 | loop fusion | bytes 1048580 | tf_op jit(solution)/shard_map/dynamic_slice | solution.py:178
  92.2 1.4 constant_dynamic-update-slice_fusion.1
  93.6 1.5 %collective-permute-start.3 = (bf16[8,256,128]{2,1,0:T(8,128)(2,1)}, bf16[8,256,128]{2,1,0:T(8,128)(2,1)}, u32[]{:S(2)}, u32[]{:S(2)}) collective-permute-start(bf16[8,256,128]{2,1,0:T(8,128)(2,1)} %get-tuple-element.14), channel_id=1, source_target_pairs={{0,1},{1,0},{2,3},{3,2},{4,5},{5,4},{6,7},{7,6},{8,9},{9,8},{10,11... | collective-permute-start | bytes 1572872 | tf_op jit(solution)/shard_map/ppermute | solution.py:51
  95.1 6.9 %collective-permute-done.5 = bf16[8,256,128]{2,1,0:T(8,128)(2,1)S(1)} collective-permute-done((bf16[8,256,128]{2,1,0:T(8,128)(2,1)}, bf16[8,256,128]{2,1,0:T(8,128)(2,1)S(1)}, u32[]{:S(2)}, u32[]{:S(2)}) %collective-permute-start.5) | collective-permute-done | bytes 524320 | tf_op jit(solution)/shard_map/ppermute | solution.py:51
  102.0 11.3 %collective-permute-done.4 = bf16[8,256,128]{2,1,0:T(8,128)(2,1)} collective-permute-done((bf16[8,256,128]{2,1,0:T(8,128)(2,1)}, bf16[8,256,128]{2,1,0:T(8,128)(2,1)}, u32[]{:S(2)}, u32[]{:S(2)}) %collective-permute-start.4) | collective-permute-done | bytes 524320 | tf_op jit(solution)/shard_map/ppermute | solution.py:51
  113.3 2.9 %fusion.10 = (f32[8,256,128]{2,1,0:T(8,128)S(1)}, f32[8,256,128]{2,1,0:T(8,128)}, f32[8,256,128]{2,1,0:T(8,128)}) fusion(f32[8,256,128]{2,1,0:T(8,128)S(1)} %get-tuple-element.27, f32[8,256,128]{2,1,0:T(8,128)S(1)} %get-tuple-element.12, bf16[8,256,128]{2,1,0:T(8,128)(2,1)S(1)} %collective-permute-done.2, ...), kind=kLoop, calls=%fused_computation.22 | loop fusion | flops 3145728 | bytes 7864324 | tf_op jit(solution)/shard_map/mul | solution.py:230
  116.3 1.6 %reduce_sum.67 = f32[8,128]{1,0:T(8,128)S(1)} reduce(f32[256,8,128]{2,1,0:T(8,128)} %bitcast.66, f32[]{:T(128)} %constant.79.clone.1), dimensions={0}, to_apply=%region_4.5 | reduce | flops 261120 | bytes 1052676 | tf_op jit(solution)/shard_map/reduce_sum | solution.py:228
  117.8 1.5 %reduce_sum.66 = f32[8,128]{1,0:T(8,128)S(1)} reduce(f32[256,8,128]{2,1,0:T(8,128)} %bitcast.65, f32[]{:T(128)} %constant.79.clone.1), dimensions={0}, to_apply=%region_3.4 | reduce | flops 261120 | bytes 1052676 | tf_op jit(solution)/shard_map/reduce_sum | solution.py:228
  120.3 2.8 %all-to-all-start.2 = ((f32[32,8,128]{2,1,0:T(8,128)}), f32[32,8,128]{2,1,0:T(8,128)S(1)}, u32[]{:S(2)}, u32[]{:S(2)}) async-start(f32[32,8,128]{2,1,0:T(8,128)} %broadcast_in_dim.5), calls=%async_computation.2 | async-start | bytes 262144 | tf_op jit(solution)/shard_map/all_to_all | solution.py:235
  123.2 8.6 %all-to-all-done.2 = f32[32,8,128]{2,1,0:T(8,128)S(1)} async-done(((f32[32,8,128]{2,1,0:T(8,128)}), f32[32,8,128]{2,1,0:T(8,128)S(1)}, u32[]{:S(2)}, u32[]{:S(2)}) %all-to-all-start.2) | async-done | bytes 131104 | tf_op jit(solution)/shard_map/all_to_all | solution.py:235
  137.2 1.3 constant_dynamic-update-slice_fusion
  139.6 4.6 %divide_convert_fusion = bf16[2,16,256,128]{3,2,1,0:T(8,128)(2,1)} fusion(bf16[2,16,256,128]{3,2,1,0:T(8,128)(2,1)S(1)} %copy-done, f32[2,16,256,128]{3,2,1,0:T(8,128)} %get-tuple-element.7, bf16[2,16,256,128]{3,2,1,0:T(8,128)(2,1)S(1)} %copy-done.1, f32[]{:T(128)} %sqrt.3, f32[]{:T(128)} %bitcast.20, f32[16,256,128]{2,1,0:T(8,128)S(1)} %convert_element_type.113), kind=kLoop, calls=%fused_computation | loop fusion | flops 8388608 | bytes 12582920 | tf_op jit(solution)/shard_map/convert_element_type | solution.py:255
  (58 shorter events, 12.5 us)
Async XLA Ops:
  0.6 18.1 %copy-start.11 = (bf16[128,128,1]{1,0,2:T(8,128)(2,1)S(1)}, bf16[128,128,1]{1,0,2:T(8,128)(2,1)}, u32[]{:S(2)}) copy-start(bf16[128,128,1]{1,0,2:T(8,128)(2,1)} %constant.105) | copy-start | bytes 98308
  3.7 15.3 %copy-start.10 = (bf16[128,128,1]{1,0,2:T(8,128)(2,1)S(1)}, bf16[128,128,1]{1,0,2:T(8,128)(2,1)}, u32[]{:S(2)}) copy-start(bf16[128,128,1]{1,0,2:T(8,128)(2,1)} %constant.104) | copy-start | bytes 98308
  3.7 15.0 %collective-permute-start.2 = (bf16[8,256,128]{2,1,0:T(8,128)(2,1)S(1)}, bf16[8,256,128]{2,1,0:T(8,128)(2,1)S(1)}, u32[]{:S(2)}, u32[]{:S(2)}) collective-permute-start(bf16[8,256,128]{2,1,0:T(8,128)(2,1)S(1)} %get-tuple-element.11), channel_id=1, source_target_pairs={{0,1},{1,0},{2,3},{3,2},{4,5},{5,4},{6,7},{7,6},{8,9},{9,8},{10,11... | collective-permute-start | bytes 1572872 | tf_op jit(solution)/shard_map/ppermute | solution.py:51
  19.0 0.9 copy-start.4
  19.0 1.2 copy-start.5
  21.9 21.0 %all-to-all-start = ((bf16[32,8,8,128]{3,2,1,0:T(8,128)(2,1)}), bf16[32,8,8,128]{3,2,1,0:T(8,128)(2,1)S(1)}, u32[]{:S(2)}, u32[]{:S(2)}) async-start(bf16[32,8,8,128]{3,2,1,0:T(8,128)(2,1)} %copy.58), calls=%async_computation | async-start | bytes 1048576 | tf_op jit(solution)/shard_map/all_to_all | solution.py:199
  45.7 45.2 %all-to-all-start.1 = ((bf16[32,8,8,128]{3,2,1,0:T(8,128)(2,1)}), bf16[32,8,8,128]{3,2,1,0:T(8,128)(2,1)S(1)}, u32[]{:S(2)}, u32[]{:S(2)}) async-start(bf16[32,8,8,128]{3,2,1,0:T(8,128)(2,1)} %bitcast.10), calls=%async_computation.1 | async-start | bytes 1048576 | tf_op jit(solution)/shard_map/all_to_all | solution.py:222
  50.5 17.1 %collective-permute-start = (bf16[2,3,256,128]{3,2,1,0:T(8,128)(2,1)S(1)}, bf16[2,3,256,128]{3,2,1,0:T(8,128)(2,1)S(1)}, u32[]{:S(2)}, u32[]{:S(2)}) collective-permute-start(bf16[2,3,256,128]{3,2,1,0:T(8,128)(2,1)S(1)} %get-tuple-element.16), channel_id=1, source_target_pairs={{0,2},{2,4},{4,6},{6,8},{8,10},{10,12},{12,14},{14,16},{16,18},{18... | collective-permute-start | bytes 1179656 | tf_op jit(solution)/shard_map/ppermute | solution.py:51
  50.8 16.8 %collective-permute-start.1 = (bf16[2,3,256,128]{3,2,1,0:T(8,128)(2,1)S(1)}, bf16[2,3,256,128]{3,2,1,0:T(8,128)(2,1)S(1)}, u32[]{:S(2)}, u32[]{:S(2)}) collective-permute-start(bf16[2,3,256,128]{3,2,1,0:T(8,128)(2,1)S(1)} %get-tuple-element.15), channel_id=1, source_target_pairs={{0,30},{2,0},{4,2},{6,4},{8,6},{10,8},{12,10},{14,12},{16,14},{18,... | collective-permute-start | bytes 1179656 | tf_op jit(solution)/shard_map/ppermute | solution.py:51
  67.6 0.8 copy-start.8
  68.4 0.8 copy-start.9
  87.0 15.0 %collective-permute-start.5 = (bf16[8,256,128]{2,1,0:T(8,128)(2,1)}, bf16[8,256,128]{2,1,0:T(8,128)(2,1)S(1)}, u32[]{:S(2)}, u32[]{:S(2)}) collective-permute-start(bf16[8,256,128]{2,1,0:T(8,128)(2,1)} %constant_dynamic-slice_fusion.1), channel_id=1, source_target_pairs={{0,1},{1,0},{2,3},{3,2},{4,5},{5,4},{6,7},{7,6},{8,9},{9,8},{10,11... | collective-permute-start | bytes 1572872 | tf_op jit(solution)/shard_map/ppermute | solution.py:51
  90.4 22.9 %collective-permute-start.4 = (bf16[8,256,128]{2,1,0:T(8,128)(2,1)}, bf16[8,256,128]{2,1,0:T(8,128)(2,1)}, u32[]{:S(2)}, u32[]{:S(2)}) collective-permute-start(bf16[8,256,128]{2,1,0:T(8,128)(2,1)} %constant_dynamic-slice_fusion), channel_id=1, source_target_pairs={{0,1},{1,0},{2,3},{3,2},{4,5},{5,4},{6,7},{7,6},{8,9},{9,8},{10,11... | collective-permute-start | bytes 1572872 | tf_op jit(solution)/shard_map/ppermute | solution.py:51
  92.2 21.2 %copy-start.6 = (bf16[16,256,128]{2,1,0:T(8,128)(2,1)S(1)}, bf16[16,256,128]{2,1,0:T(8,128)(2,1)}, u32[]{:S(2)}) copy-start(bf16[16,256,128]{2,1,0:T(8,128)(2,1)} %get-tuple-element.9) | copy-start | bytes 3145732
  92.2 21.2 %copy-start.7 = (bf16[16,256,128]{2,1,0:T(8,128)(2,1)S(1)}, bf16[16,256,128]{2,1,0:T(8,128)(2,1)}, u32[]{:S(2)}) copy-start(bf16[16,256,128]{2,1,0:T(8,128)(2,1)} %get-tuple-element.10) | copy-start | bytes 3145732
  93.6 19.7 %copy-start.2 = (bf16[16,256,128]{2,1,0:T(8,128)(2,1)}, bf16[16,256,128]{2,1,0:T(8,128)(2,1)S(1)}, u32[]{:S(2)}) copy-start(bf16[16,256,128]{2,1,0:T(8,128)(2,1)S(1)} %get-tuple-element.13) | copy-start | bytes 3145732
  93.6 43.5 %collective-permute-start.3 = (bf16[8,256,128]{2,1,0:T(8,128)(2,1)}, bf16[8,256,128]{2,1,0:T(8,128)(2,1)}, u32[]{:S(2)}, u32[]{:S(2)}) collective-permute-start(bf16[8,256,128]{2,1,0:T(8,128)(2,1)} %get-tuple-element.14), channel_id=1, source_target_pairs={{0,1},{1,0},{2,3},{3,2},{4,5},{5,4},{6,7},{7,6},{8,9},{9,8},{10,11... | collective-permute-start | bytes 1572872 | tf_op jit(solution)/shard_map/ppermute | solution.py:51
  116.3 3.4 %copy-start.12 = (f32[4,8,128]{2,1,0:T(8,128)S(1)}, f32[4,8,128]{2,1,0:T(8,128)}, u32[]{:S(2)}) copy-start(f32[4,8,128]{2,1,0:T(8,128)} %get-tuple-element.8) | copy-start | bytes 49156
  116.3 20.9 %copy-start.3 = (bf16[16,256,128]{2,1,0:T(8,128)(2,1)S(1)}, bf16[16,256,128]{2,1,0:T(8,128)(2,1)}, u32[]{:S(2)}) copy-start(bf16[16,256,128]{2,1,0:T(8,128)(2,1)} %copy-done.2) | copy-start | bytes 3145732
  120.3 11.4 %all-to-all-start.2 = ((f32[32,8,128]{2,1,0:T(8,128)}), f32[32,8,128]{2,1,0:T(8,128)S(1)}, u32[]{:S(2)}, u32[]{:S(2)}) async-start(f32[32,8,128]{2,1,0:T(8,128)} %broadcast_in_dim.5), calls=%async_computation.2 | async-start | bytes 262144 | tf_op jit(solution)/shard_map/all_to_all | solution.py:235
  137.2 1.8 %copy-start = (bf16[2,16,256,128]{3,2,1,0:T(8,128)(2,1)S(1)}, bf16[2,16,256,128]{3,2,1,0:T(8,128)(2,1)}, u32[]{:S(2)}) copy-start(bf16[2,16,256,128]{3,2,1,0:T(8,128)(2,1)} %current.1) | copy-start | bytes 6291460
  137.2 2.4 %copy-start.1 = (bf16[2,16,256,128]{3,2,1,0:T(8,128)(2,1)S(1)}, bf16[2,16,256,128]{3,2,1,0:T(8,128)(2,1)}, u32[]{:S(2)}) copy-start(bf16[2,16,256,128]{3,2,1,0:T(8,128)(2,1)} %orbitals.1) | copy-start | bytes 6291460
where the time goes:
time: 147 us; the launch traced here: 146 us
  waiting for transfers between devices  65.5 us (45%)
  starting transfers between devices  23.6 us (16%)
  Pallas kernels  15.9 us (11%)
  other arithmetic  14.4 us (10%)
  local copies, waits for them, and re-layouts  13.5 us (9%)
  between operations  8.44 us (6%)
  matrix products  5.12 us (3%)
    ppermute x6, waiting for transfers between devices, shifted(): lax.ppermute(array, axis, [(i, (i + step) % size) for i in range(size)])  42.1 us
    pallas_call x1, Pallas kernels, stencil(): pl.pallas_call(stencil_body, grid=(planes,), in_specs=[smem, smem, reside...  15.9 us
    all_to_all x2, waiting for transfers between devices, split_step(): lax.all_to_all(spectrum, both, split_axis=0, concat_axis=0, tiled=True)  14.8 us
    ppermute x6, starting transfers between devices, shifted(): lax.ppermute(array, axis, [(i, (i + step) % size) for i in range(size)])  11.1 us
    all_to_all x2, starting transfers between devices, split_step(): lax.all_to_all(spectrum, both, split_axis=0, concat_axis=0, tiled=True)  9.68 us
    all_to_all x1, waiting for transfers between devices, split_step(): lax.all_to_all(partial, both, split_axis=0, concat_axis=0, tiled=True)  8.57 us
    dot_general x12, matrix products, product(): jnp.einsum(spec, part, values, preferred_element_type=jnp.float32)  5.12 us
    convert_element_type x1, other arithmetic, split_step(): next_vector = (remainder / norm_next).astype(jnp.bfloat16)  4.65 us
  transfers between devices with their start and end apart: 9, of which 6 were waited for; matrix products, arithmetic and copies ran while one was open for 11% of the time, Pallas kernels for 11%

commit v1 on v0

--- a/solution.py
+++ b/solution.py
@@ -40,18 +40,250 @@
     return wavenumber * wavenumber
 
 
-def product(spec, table, values):
-    values = values.astype(jnp.bfloat16)
-    parts = two_parts(table)
-    return sum(jnp.einsum(spec, part, values, preferred_element_type=jnp.float32) for part in parts)
-
-
 def shifted(array, axis, step):
     size = lax.axis_size(axis)
     return lax.ppermute(array, axis, [(i, (i + step) % size) for i in range(size)])
 
 
+def dot(left, right):
+    return jnp.dot(left, right, preferred_element_type=jnp.float32)
+
+
+def resident(array):
+    return pl.BlockSpec(array.shape, lambda *_, n=len(array.shape): (0,) * n)
+
+
+def struct(shape, dtype):
+    return jax.ShapeDtypeStruct(shape, dtype)
+
+
+def in_smem():
+    return pl.BlockSpec(memory_space=pltpu.SMEM)
+
+
+def in_vmem():
+    return pl.BlockSpec(memory_space=pltpu.VMEM)
+
+
+def cost(flops, moved):
+    return pl.CostEstimate(flops=int(flops), bytes_accessed=int(moved), transcendentals=0)
+
+
+def stacked_rows(table):
+    return jnp.concatenate(two_parts(table), axis=0)
+
+
+def density_body(first, orbitals, current, density, weight):
+    fields = orbitals.shape[0]
+    total = None
+    square = None
+    for i in range(fields):
+        orbital = orbitals[i].astype(jnp.float32)
+        term = orbital * current[i].astype(jnp.float32)
+        total = term if total is None else total + term
+        square = orbital * orbital if square is None else square + orbital * orbital
+    density[...] = total.astype(density.dtype)
+    weight[...] = square.astype(weight.dtype)
+
+
+def density_of(index, own, orbitals, lanczos, dtype):
+    fields, _, length_y, length_z = lanczos.shape
+    step = 2 if own % 2 == 0 else 1
+    first = jnp.reshape(index * (own // step), (1,)).astype(jnp.int32)
+    fields_spec = pl.BlockSpec((fields, step, length_y, length_z), lambda a, f: (0, f[0] + a, 0, 0))
+    plane_spec = pl.BlockSpec((step, length_y, length_z), lambda a, f: (a, 0, 0))
+    points = own * length_y * length_z
+    return pl.pallas_call(
+        density_body,
+        grid_spec=pltpu.PrefetchScalarGridSpec(
+            num_scalar_prefetch=1,
+            grid=(own // step,),
+            in_specs=[fields_spec, fields_spec],
+            out_specs=[plane_spec, plane_spec],
+        ),
+        out_shape=[struct((own, length_y, length_z), dtype), struct((own, length_y, length_z), dtype)],
+        cost_estimate=cost(points * fields * 4, points * (fields * 4 + 8)),
+        name="density",
+    )(first, orbitals, lanczos)
+
+
+def lateral_body(*refs):
+    *terms, table_y, table_y_low, table_z, density, spectrum = refs
+    own, _, length_z = density.shape
+    devices, _, modes_y, _ = spectrum.shape
+    for p in range(own):
+        total = terms[0][p].astype(jnp.float32)
+        for term in terms[1:]:
+            total = total + term[p].astype(jnp.float32)
+        density[p] = total
+        narrow = total.astype(jnp.bfloat16)
+        value = dot(jnp.concatenate([narrow, narrow], axis=1), table_z[...]).astype(jnp.bfloat16)
+        value = dot(table_y[...], value) + dot(table_y_low[...], value)
+        spectrum[:, p] = value.reshape(devices, modes_y, length_z).astype(spectrum.dtype)
+
+
+def lateral(terms, devices, table_y, table_z):
+    own, length_y, length_z = terms[0].shape
+    modes_y = length_y // devices
+    tables = two_parts(table_y) + (stacked_rows(table_z),)
+    points = own * length_y * length_z
+    return pl.pallas_call(
+        lateral_body,
+        in_specs=[in_vmem()] * (len(terms) + 3),
+        out_specs=[in_vmem(), in_vmem()],
+        out_shape=[
+            struct((own, length_y, length_z), jnp.float32),
+            struct((devices, own, modes_y, length_z), jnp.bfloat16),
+        ],
+        cost_estimate=cost(points * 4 * (length_y + length_z), points * 8),
+        name="lateral",
+    )(*terms, *tables)
+
+
+def filter_body(spectrum, kernel, table_x, table_x_low, filtered, rows):
+    devices, own, modes_y, length_z = spectrum.shape
+    length_x = devices * own
+    wide = spectrum[...].astype(jnp.float32)
+    rows[...] = wide.reshape(length_x * modes_y, length_z)
+    for b in range(modes_y):
+        place = pl.ds(b, length_x, stride=modes_y)
+        value = rows[place, :].astype(jnp.bfloat16)
+        value = dot(table_x[...], value) + dot(table_x_low[...], value)
+        value = (value * kernel[b]).astype(jnp.bfloat16)
+        rows[place, :] = dot(table_x[...], value) + dot(table_x_low[...], value)
+    filtered[...] = rows[...].reshape(filtered.shape).astype(filtered.dtype)
+
+
+def filtered_of(spectrum, kernel, table_x):
+    devices, own, modes_y, length_z = spectrum.shape
+    length_x = devices * own
+    points = spectrum.size
+    return pl.pallas_call(
+        filter_body,
+        in_specs=[in_vmem()] * 4,
+        out_specs=in_vmem(),
+        out_shape=struct(spectrum.shape, spectrum.dtype),
+        scratch_shapes=[pltpu.VMEM((length_x * modes_y, length_z), jnp.float32)],
+        cost_estimate=cost(points * 8 * length_x, points * 8),
+        name="filter",
+    )(spectrum, kernel, *two_parts(table_x))
+
+
+def inverse_body(*refs):
+    groups = (len(refs) - 8) // 2
+    spectrum, density, early, table_y, table_y_low, table_z = refs[:6]
+    crosses, weights = refs[6 : 6 + groups], refs[6 + groups : 6 + 2 * groups]
+    potential, partial = refs[6 + 2 * groups :]
+    devices, own, modes_y, length_z = spectrum.shape
+    length_y = devices * modes_y
+
+    def folded(values):
+        return jnp.sum(values.reshape(length_y // 8, 8, length_z), axis=0)
+
+    totals = [jnp.zeros((8, length_z), jnp.float32) for _ in range(3)]
+    for p in range(own):
+        value = spectrum[:, p].astype(jnp.float32).reshape(length_y, length_z).astype(jnp.bfloat16)
+        value = (dot(table_y[...], value) + dot(table_y_low[...], value)).astype(jnp.bfloat16)
+        value = dot(jnp.concatenate([value, value], axis=1), table_z[...])
+        potential[p] = value.astype(potential.dtype)
+        cross = sum(ref[p].astype(jnp.float32) for ref in crosses)
+        weight = sum(ref[p].astype(jnp.float32) for ref in weights)
+        for j, term in enumerate((density[p] * value, cross * value, weight * value * value)):
+            totals[j] = totals[j] + folded(term)
+    rows = [jnp.sum(early[j], axis=0, keepdims=True) for j in range(4)]
+    rows = rows + [jnp.sum(total, axis=0, keepdims=True) for total in totals]
+    rows = jnp.concatenate(rows + [jnp.zeros((1, length_z), jnp.float32)], axis=0)
+    partial[...] = jnp.broadcast_to(rows[None], partial.shape)
+
+
+def inverse(spectrum, density, early, crosses, weights, table_y, table_z):
+    devices, own, modes_y, length_z = spectrum.shape
+    length_y = devices * modes_y
+    tables = two_parts(table_y) + (stacked_rows(table_z),)
+    points = spectrum.size
+    return pl.pallas_call(
+        inverse_body,
+        in_specs=[in_vmem()] * (6 + len(crosses) + len(weights)),
+        out_specs=[in_vmem(), in_vmem()],
+        out_shape=[
+            struct((own, length_y, length_z), jnp.bfloat16),
+            struct((devices, 8, length_z), jnp.float32),
+        ],
+        cost_estimate=cost(points * 4 * (length_y + length_z), points * 16),
+        name="inverse",
+    )(spectrum, density, early, *tables, *crosses, *weights)
+
+
+def final_body(entries, groups, turn, moments, fixed, orbitals, current, *refs):
+    potentials = refs[:groups]
+    following, rayleigh_out, norm_out, scalars = refs[groups:]
+    step = pl.program_id(0)
+    own = pl.num_programs(0) // groups
+    fields = fixed.shape[0]
+    length_z = fixed.shape[3]
+
+    @pl.when(step == 0)
+    def _():
+        means = jnp.sum(jnp.sum(moments[...], axis=0), axis=1, keepdims=True) / entries
+        value, rest, square, self_mean, density, cross, weight = (means[j : j + 1] for j in range(7))
+        rayleigh = value + density
+        squares = square + 2.0 * cross + weight
+        squares = squares - 2.0 * rayleigh * (rest + density) + rayleigh * rayleigh * self_mean
+        norm = jnp.sqrt(squares + 1e-06)
+        scalars[0:1, :] = jnp.broadcast_to(rayleigh, (1, length_z))
+        scalars[1:2, :] = jnp.broadcast_to(1.0 / norm, (1, length_z))
+        rayleigh_out[0] = jnp.sum(rayleigh)
+        norm_out[0] = jnp.sum(norm)
+
+    for part in range(groups):
+
+        @pl.when(jnp.logical_and(step >= part * own, step < (part + 1) * own))
+        def _(part=part):
+            potential = potentials[part][0].astype(jnp.float32)
+            for i in range(fields):
+                image = fixed[i, 0] + orbitals[i, 0].astype(jnp.float32) * potential
+                image = image - scalars[0:1, :] * current[i, 0].astype(jnp.float32)
+                following[i, 0] = (image * scalars[1:2, :]).astype(following.dtype)
+
+
+def final(turn, moments, fixed, orbitals, lanczos, potentials, entries):
+    fields, planes, length_y, length_z = lanczos.shape
+    groups = len(potentials)
+    own = planes // groups
+    field_spec = pl.BlockSpec(
+        (fields, 1, length_y, length_z), lambda a, t: (0, lax.rem(a + t[0], planes), 0, 0)
+    )
+    part_specs = [
+        pl.BlockSpec(
+            (1, length_y, length_z),
+            lambda a, t, part=part: (jnp.clip(a - part * own, 0, own - 1), 0, 0),
+        )
+        for part in range(groups)
+    ]
+    points = fields * planes * length_y * length_z
+    return pl.pallas_call(
+        functools.partial(final_body, entries, groups),
+        grid_spec=pltpu.PrefetchScalarGridSpec(
+            num_scalar_prefetch=1,
+            grid=(planes,),
+            in_specs=[in_vmem(), field_spec, field_spec, field_spec] + part_specs,
+            out_specs=[field_spec, in_smem(), in_smem()],
+            scratch_shapes=[pltpu.VMEM((8, length_z), jnp.float32)],
+        ),
+        out_shape=[
+            struct(lanczos.shape, jnp.bfloat16),
+            struct((1,), jnp.float32),
+            struct((1,), jnp.float32),
+        ],
+        compiler_params=pltpu.CompilerParams(dimension_semantics=("arbitrary",)),
+        cost_estimate=cost(points * 5, points * 11),
+        name="final",
+    )(turn, moments, fixed, orbitals, lanczos, *potentials)
+
+
 def stencil_body(
+    groups,
+    turn,
     energies,
     beta,
     before,
@@ -63,26 +295,25 @@
     band_y,
     band_y_low,
     band_z,
-    band_z_low,
     fixed,
-    cross,
-    weight,
     sums,
-    extended,
+    *refs,
 ):
-    plane = pl.program_id(0)
+    crosses, extended = refs[:groups], refs[groups]
+    step = pl.program_id(0)
     fields, planes, length_y, length_z = current.shape
+    own = planes // groups
     half = [-0.5 * w for w in side_weights]
     rows = 64
 
-    @pl.when(plane == 0)
+    @pl.when(step == 0)
     def _():
         extended[:, :reach_max] = before[...]
         extended[:, reach_max : reach_max + planes] = current[...]
         extended[:, reach_max + planes :] = after[...]
         sums[...] = jnp.zeros_like(sums)
 
-    here = plane + reach_max
+    here = lax.rem(step + turn[0], planes) + reach_max
     beta_now = beta[0]
 
     def folded(values):
@@ -93,13 +324,11 @@
         piece = pl.ds(start, rows)
         local = local_potential[0, piece, :]
         cross_now = jnp.zeros((rows, length_z), jnp.float32)
-        weight_now = jnp.zeros((rows, length_z), jnp.float32)
         for i in range(fields):
             whole = extended[i, here]
             narrow = extended[i, here, piece, :]
-            dot = functools.partial(jnp.dot, preferred_element_type=jnp.float32)
             value = dot(band_y[piece, :], whole) + dot(band_y_low[piece, :], whole)
-            value = value + dot(narrow, band_z[...]) + dot(narrow, band_z_low[...])
+            value = value + dot(jnp.concatenate([narrow, narrow], axis=1), band_z[...])
             for offset in range(reach_max):
                 right = extended[i, here + offset + 1, piece, :].astype(jnp.float32)
                 left = extended[i, here - offset - 1, piece, :].astype(jnp.float32)
@@ -111,56 +340,57 @@
             rest = value - beta_now * older
             fixed[i, 0, piece, :] = rest
             cross_now = cross_now + orbital * rest
-            weight_now = weight_now + orbital * orbital
             for j, term in enumerate((centre * value, centre * rest, rest * rest, centre * centre)):
                 totals[j] = totals[j] + folded(term)
-        cross[0, piece, :] = cross_now.astype(cross.dtype)
-        weight[0, piece, :] = weight_now.astype(weight.dtype)
+        for part in range(groups):
+
+            @pl.when(jnp.logical_and(step >= part * own, step < (part + 1) * own))
+            def _(part=part, piece=piece, cross_now=cross_now):
+                crosses[part][0, piece, :] = cross_now.astype(crosses[part].dtype)
+
     for j in range(4):
         sums[j] += totals[j]
 
 
-def stencil(energies, beta, before, current, after, orbitals, previous, local_potential):
-    fields, planes, length_y, length_z = current.shape
+def stencil(turn, groups, energies, beta, before, lanczos, after, orbitals, previous, local_potential):
+    fields, planes, length_y, length_z = lanczos.shape
+    own = planes // groups
     tables = two_parts(-0.5 * band_matrix(length_y, 3.0 * central_weight))
-    tables = tables + two_parts(-0.5 * band_matrix(length_z, 0.0))
-    smem = pl.BlockSpec(memory_space=pltpu.SMEM)
-
-    def resident(array):
-        return pl.BlockSpec(array.shape, lambda a, n=array.ndim: (0,) * n)
-
-    field_spec = pl.BlockSpec((fields, 1, length_y, length_z), lambda a: (0, a, 0, 0))
-    plane_spec = pl.BlockSpec((1, length_y, length_z), lambda a: (a, 0, 0))
+    tables = tables + (stacked_rows(-0.5 * band_matrix(length_z, 0.0)),)
+    field_spec = pl.BlockSpec(
+        (fields, 1, length_y, length_z), lambda a, t: (0, lax.rem(a + t[0], planes), 0, 0)
+    )
+    plane_spec = pl.BlockSpec((1, length_y, length_z), lambda a, t: (lax.rem(a + t[0], planes), 0, 0))
+    part_specs = [
+        pl.BlockSpec(
+            (1, length_y, length_z),
+            lambda a, t, part=part: (jnp.clip(a - part * own, 0, own - 1), 0, 0),
+        )
+        for part in range(groups)
+    ]
     points = planes * length_y * length_z
     return pl.pallas_call(
-        stencil_body,
-        grid=(planes,),
-        in_specs=[smem, smem, resident(before), resident(current), resident(after)]
-        + [field_spec, field_spec, plane_spec]
-        + [resident(table) for table in tables],
-        out_specs=[
-            field_spec,
-            plane_spec,
-            plane_spec,
-            pl.BlockSpec((4, 8, length_z), lambda a: (0, 0, 0)),
-        ],
+        functools.partial(stencil_body, groups),
+        grid_spec=pltpu.PrefetchScalarGridSpec(
+            num_scalar_prefetch=1,
+            grid=(planes,),
+            in_specs=[in_smem(), in_smem(), in_vmem(), resident(lanczos), in_vmem()]
+            + [field_spec, field_spec, plane_spec]
+            + [in_vmem()] * 3,
+            out_specs=[field_spec, pl.BlockSpec((4, 8, length_z), lambda a, t: (0, 0, 0))] + part_specs,
+            scratch_shapes=[
+                pltpu.VMEM((fields, planes + 2 * reach_max, length_y, length_z), lanczos.dtype)
+            ],
+        ),
         out_shape=[
-            jax.ShapeDtypeStruct(current.shape, jnp.float32),
-            jax.ShapeDtypeStruct((planes, length_y, length_z), jnp.bfloat16),
-            jax.ShapeDtypeStruct((planes, length_y, length_z), jnp.bfloat16),
-            jax.ShapeDtypeStruct((4, 8, length_z), jnp.float32),
-        ],
-        scratch_shapes=[
-            pltpu.VMEM((fields, planes + 2 * reach_max, length_y, length_z), current.dtype)
-        ],
+            struct(lanczos.shape, jnp.float32),
+            struct((4, 8, length_z), jnp.float32),
+        ]
+        + [struct((own, length_y, length_z), jnp.bfloat16)] * groups,
         compiler_params=pltpu.CompilerParams(dimension_semantics=("arbitrary",)),
-        cost_estimate=pl.CostEstimate(
-            flops=points * fields * 2 * 2 * (length_y + length_z),
-            bytes_accessed=points * (fields * 10 + 8),
-            transcendentals=0,
-        ),
+        cost_estimate=cost(points * fields * 4 * (length_y + length_z), points * (fields * 10 + 8)),
         name="stencil",
-    )(energies, beta, before, current, after, orbitals, previous, local_potential, *tables)
+    )(turn, energies, beta, before, lanczos, after, orbitals, previous, local_potential, *tables)
 
 
 def split_step(orbitals, energies, local_potential, lanczos, previous, beta):
@@ -173,87 +403,45 @@
     modes_y = length_y // devices
     me = lax.axis_index("orb")
     both = ("dom", "orb")
-
-    def part(array, index, dim):
-        return lax.dynamic_slice_in_dim(array, index * own, own, axis=dim)
-
-    def density_of(index):
-        first = part(orbitals, index, 1).astype(jnp.float32)
-        return jnp.sum(first * part(lanczos, index, 1).astype(jnp.float32), axis=0)
-
-    def gathered_sum(local_of, mine):
-        total = mine
-        for step in range(1, groups):
-            sent = local_of((me + step) % groups).astype(jnp.bfloat16)
-            total = total + shifted(sent, "orb", step).astype(jnp.float32)
-        return total
-
-    density = gathered_sum(density_of, density_of(me))
+    table_x, table_y, table_z = (cas_matrix(n) for n in (length_x, length_y, length_z))
+    turn = jnp.reshape(((me + 1) % groups) * own, (1,)).astype(jnp.int32)
+
+    def part_of(step):
+        return (me + step) % groups
+
+    parts = [density_of(part_of(step), own, orbitals, lanczos, jnp.bfloat16) for step in range(1, groups)]
+    received = [shifted(parts[step - 1][0], "orb", step) for step in range(1, groups)]
     before = shifted(lanczos[:, planes - reach_max :], "dom", 1)
     after = shifted(lanczos[:, :reach_max], "dom", -1)
-
-    table_x, table_y, table_z = (cas_matrix(n) for n in (length_x, length_y, length_z))
-    spectrum = product("cz,ayz->ayc", table_z, density)
-    spectrum = product("by,ayc->abc", table_y, spectrum).astype(jnp.bfloat16)
-    spectrum = spectrum.reshape(own, devices, modes_y, length_z).transpose(1, 0, 2, 3)
-    spectrum = lax.all_to_all(spectrum, both, split_axis=0, concat_axis=0, tiled=True)
-    spectrum = spectrum.reshape(length_x, modes_y, length_z)
-
-    fixed, cross, weight, sums = stencil(
-        energies, beta, before, lanczos, after, orbitals, previous, local_potential
-    )
-
-    def planes_sum(array):
-        return gathered_sum(lambda i: part(array, i, 0), part(array, me, 0).astype(jnp.float32))
-
-    weight = planes_sum(weight)
-    cross = planes_sum(cross)
-
-    square_x = wave_square(jnp.arange(length_x, dtype=jnp.int32), length_x)
+    density, weight = density_of(me, own, orbitals, lanczos, jnp.float32)
+
     index = lax.axis_index("dom") * groups + me
     index_y = index * modes_y + jnp.arange(modes_y, dtype=jnp.int32)
+    square_x = wave_square(jnp.arange(length_x, dtype=jnp.int32), length_x)
     square_y = wave_square(index_y, length_y)
     square_z = wave_square(jnp.arange(length_z, dtype=jnp.int32), length_z)
-    summed = square_x[:, None, None] + square_y[None, :, None] + square_z[None, None, :] + screening
-    normalizer = 4.0 * jnp.pi / (length_x * length_y * length_z)
-    spectrum = product("ax,xbc->abc", table_x, spectrum) * (normalizer / summed)
-    spectrum = product("ax,xbc->abc", table_x, spectrum).astype(jnp.bfloat16)
-    spectrum = spectrum.reshape(devices, own, modes_y, length_z)
+    summed = square_x[None, :, None] + square_y[:, None, None] + square_z[None, None, :] + screening
+    kernel = 4.0 * jnp.pi / (length_x * length_y * length_z) / summed
+
+    density, spectrum = lateral([density] + received, devices, table_y, table_z)
     spectrum = lax.all_to_all(spectrum, both, split_axis=0, concat_axis=0, tiled=True)
-    spectrum = spectrum.transpose(1, 0, 2, 3).reshape(own, length_y, length_z)
-    spectrum = product("by,ayz->abz", table_y, spectrum)
-    potential = product("cz,abz->abc", table_z, spectrum)
-
-    def lanes(values):
-        return jnp.sum(values.reshape(-1, 8, length_z), axis=0)
-
-    late = [lanes(density * potential), lanes(cross * potential), lanes(weight * potential * potential)]
-    partial = jnp.concatenate([sums, jnp.stack(late)], axis=0)
-    partial = jnp.sum(partial, axis=1)
-    partial = jnp.concatenate([partial, jnp.zeros((1, length_z), jnp.float32)], axis=0)
-    partial = jnp.broadcast_to(partial[None], (devices,) + partial.shape)
-    partial = lax.all_to_all(partial, both, split_axis=0, concat_axis=0, tiled=True)
-    moments = jnp.sum(partial, axis=(0, 2))
-
-    narrow = potential.astype(jnp.bfloat16)
-    whole = jnp.zeros((planes, length_y, length_z), jnp.bfloat16)
-    whole = lax.dynamic_update_slice_in_dim(whole, narrow, me * own, 0)
-    for step in range(1, groups):
-        source = (me - step) % groups
-        whole = lax.dynamic_update_slice_in_dim(whole, shifted(narrow, "orb", step), source * own, 0)
-    image = fixed + orbitals.astype(jnp.float32) * whole.astype(jnp.float32)[None]
-
+    weights = [shifted(parts[step - 1][1], "orb", step) for step in range(1, groups)]
+    fixed, early, *crosses = stencil(
+        turn, groups, energies, beta, before, lanczos, after, orbitals, previous, local_potential
+    )
+    arrived = [shifted(crosses[step - 1], "orb", step) for step in range(1, groups)]
+
+    spectrum = filtered_of(spectrum, kernel, table_x)
+    spectrum = lax.all_to_all(spectrum, both, split_axis=0, concat_axis=0, tiled=True)
+    potential, partial = inverse(
+        spectrum, density, early, [crosses[-1]] + arrived, [weight] + weights, table_y, table_z
+    )
+    potentials = [shifted(potential, "orb", -step) for step in range(1, groups)]
+    moments = lax.all_to_all(partial, both, split_axis=0, concat_axis=0, tiled=True)
     entries = float(fields * groups * length_x * length_y * length_z)
-    value_mean, rest_mean, square_mean, self_mean, density_mean, cross_mean, weight_mean = (
-        moments[j] / entries for j in range(7)
-    )
-    rayleigh = value_mean + density_mean
-    squares = square_mean + 2.0 * cross_mean + weight_mean
-    squares = squares - 2.0 * rayleigh * (rest_mean + density_mean) + rayleigh * rayleigh * self_mean
-    norm_next = jnp.sqrt(squares + 1e-06)
-    remainder = image - rayleigh * lanczos.astype(jnp.float32)
-    next_vector = (remainder / norm_next).astype(jnp.bfloat16)
-    return (next_vector, jnp.reshape(rayleigh, (1,)), jnp.reshape(norm_next, (1,)))
+    return tuple(
+        final(turn, moments, fixed, orbitals, lanczos, potentials + [potential], entries)
+    )
 
 
 def extended(array, sides, width):
@@ -355,7 +543,7 @@
 
 
 def per_device(orbitals, energies, local_potential, lanczos, previous, beta):
-    fields, planes, length_y, length_z = lanczos.shape
+    _, planes, length_y, length_z = lanczos.shape
     groups = lax.axis_size("orb")
     devices = groups * lax.axis_size("dom")
     fits = planes % groups == 0 and planes >= reach_max

time: 147 us -> 130 us (0.88)
  Pallas kernels: 15.9 us -> 52.5 us
  waiting for transfers between devices: 65.5 us -> 30.2 us
  blocking collectives: 0 us -> 14.4 us
  other arithmetic: 14.4 us -> 1.42 us
  local copies, waits for them, and re-layouts: 13.5 us -> 5.45 us
  between operations: 8.44 us -> 1.39 us
  matrix products: 5.12 us -> 0 us
    pallas_call x1 -> x7, Pallas kernels: 15.9 us -> 52.5 us  [the longest x1 19.5 us: stencil(): pl.pallas_call(functools.partial(stencil_body, groups), grid_spec=pltpu.P...]
    ppermute x6, waiting for transfers between devices: 42.1 us -> 21.9 us  [shifted(): lax.ppermute(array, axis, [(i, (i + step) % size) for i in range(size)])]
    all_to_all x0 -> x1, blocking collectives: none -> 14.4 us  [split_step(): lax.all_to_all(partial, both, split_axis=0, concat_axis=0, tiled=True)]
    all_to_all x1 -> x0, waiting for transfers between devices: 8.57 us -> none  [split_step(): lax.all_to_all(partial, both, split_axis=0, concat_axis=0, tiled=True)]
    all_to_all x2, waiting for transfers between devices: 14.8 us -> 8.26 us  [split_step(): lax.all_to_all(spectrum, both, split_axis=0, concat_axis=0, tiled=True)]
    reduce_sum x6 -> x0, other arithmetic: 6.55 us -> none  [the longest x3 3.35 us: lanes(): return jnp.sum(values.reshape(-1, 8, length_z), axis=0)]
    dot_general x12 -> x0, matrix products: 5.12 us -> none  [product(): jnp.einsum(spec, part, values, preferred_element_type=jnp.float32)]
    convert_element_type x2 -> x0, other arithmetic: 4.85 us -> none  [the longest x1 4.65 us: split_step(): next_vector = (remainder / norm_next).astype(jnp.bfloat16)]
  transfers between devices with their start and end apart: 9 -> 8, of which waited for: 6 -> 3; matrix products, arithmetic and copies ran while one was open for 11% -> 2% of each run, Pallas kernels for 11% -> 22%
where the time goes in v1:
time: 130 us; the launch traced here: 129 us
  Pallas kernels  52.5 us (40%)
  waiting for transfers between devices  30.2 us (23%)
  starting transfers between devices  23.2 us (18%)
  blocking collectives  14.4 us (11%)
  local copies, waits for them, and re-layouts  5.45 us (4%)
  other arithmetic  1.42 us (1%)
  between operations  1.39 us (1%)
    ppermute x6, waiting for transfers between devices, shifted(): lax.ppermute(array, axis, [(i, (i + step) % size) for i in range(size)])  21.9 us
    pallas_call x1, Pallas kernels, stencil(): pl.pallas_call(functools.partial(stencil_body, groups), grid_spec=pltpu.P...  19.5 us
    all_to_all x1, blocking collectives, split_step(): lax.all_to_all(partial, both, split_axis=0, concat_axis=0, tiled=True)  14.4 us
    all_to_all x2, starting transfers between devices, split_step(): lax.all_to_all(spectrum, both, split_axis=0, concat_axis=0, tiled=True)  13.3 us
    pallas_call x1, Pallas kernels, final(): pl.pallas_call(functools.partial(final_body, entries, groups), grid_spec=...  11.3 us
    ppermute x6, starting transfers between devices, shifted(): lax.ppermute(array, axis, [(i, (i + step) % size) for i in range(size)])  9.84 us
    all_to_all x2, waiting for transfers between devices, split_step(): lax.all_to_all(spectrum, both, split_axis=0, concat_axis=0, tiled=True)  8.26 us
    pallas_call x2, Pallas kernels, density_of(): pl.pallas_call(density_body, grid_spec=pltpu.PrefetchScalarGridSpec(num_s...  7.52 us
  transfers between devices with their start and end apart: 8, of which 3 were waited for; matrix products, arithmetic and copies ran while one was open for 2% of the time, Pallas kernels for 22%

profile of v1, /device:TPU:0, one launch (start us, length us, event | category | flops | bytes accessed | tf_op | source)
XLA Modules:
  0.0 128.5 jit_solution(14490885267151305209)
XLA Ops:
  0.6 3.7 %density.3 = (bf16[8,256,128]{2,1,0:T(8,128)(2,1)}, bf16[8,256,128]{2,1,0:T(8,128)(2,1)}) custom-call(s32[1]{0:T(128)} %bitcast.2.first, bf16[2,16,256,128]{3,2,1,0:T(8,128)(2,1)} %orbitals.7, bf16[2,16,256,128]{3,2,1,0:T(8,128)(2,1)} %current.7), custom_call_target="tpu_custom_call" | custom-call | flops 2097152 | bytes 4194304 | tf_op jit(solution)/shard_map/density/pallas_call | solution.py:96
  4.3 3.0 %collective-permute-start = (bf16[8,256,128]{2,1,0:T(8,128)(2,1)}, bf16[8,256,128]{2,1,0:T(8,128)(2,1)S(1)}, u32[]{:S(2)}, u32[]{:S(2)}) collective-permute-start(bf16[8,256,128]{2,1,0:T(8,128)(2,1)} %get-tuple-element.16), channel_id=1, source_target_pairs={{0,1},{1,0},{2,3},{3,2},{4,5},{5,4},{6,7},{7,6},{8,9},{9,8},{10,11... | collective-permute-start | bytes 1572872 | tf_op jit(solution)/shard_map/ppermute | solution.py:45
  7.3 3.8 %density.2 = (f32[8,256,128]{2,1,0:T(8,128)}, f32[8,256,128]{2,1,0:T(8,128)}) custom-call(s32[1]{0:T(128)} %bitcast.1.first, bf16[2,16,256,128]{3,2,1,0:T(8,128)(2,1)} %orbitals.7, bf16[2,16,256,128]{3,2,1,0:T(8,128)(2,1)} %current.7), custom_call_target="tpu_custom_call" | custom-call | flops 2097152 | bytes 4194304 | tf_op jit(solution)/shard_map/density/pallas_call | solution.py:96
  11.2 8.3 %collective-permute-done.refs_1_ = bf16[8,256,128]{2,1,0:T(8,128)(2,1)S(1)} collective-permute-done((bf16[8,256,128]{2,1,0:T(8,128)(2,1)}, bf16[8,256,128]{2,1,0:T(8,128)(2,1)S(1)}, u32[]{:S(2)}, u32[]{:S(2)}) %collective-permute-start) | collective-permute-done | bytes 524320 | tf_op jit(solution)/shard_map/ppermute | solution.py:45
  19.5 0.8 copy-done.5
  20.3 4.5 %lateral.1 = (f32[8,256,128]{2,1,0:T(8,128)}, bf16[32,8,8,128]{3,2,1,0:T(8,128)(2,1)}) custom-call(f32[8,256,128]{2,1,0:T(8,128)} %get-tuple-element.15.refs_0_, bf16[8,256,128]{2,1,0:T(8,128)(2,1)} %copy-done.5, bf16[256,256]{1,0:T(8,128)(2,1)} %constant.58.clone.refs_2_.table_x.refs_3_, bf16[256,256]{1,0:T(8,128)(2,1)} %constant.59.clone.refs_3_.table_x_low.refs_4_, ...), custom_call_target="tpu_custom_call" | custom-call | flops 402653184 | bytes 2097152 | tf_op jit(solution)/shard_map/lateral/pallas_call | solution.py:130
  24.8 6.1 %all-to-all-start = ((bf16[32,8,8,128]{3,2,1,0:T(8,128)(2,1)}), bf16[32,8,8,128]{3,2,1,0:T(8,128)(2,1)S(1)}, u32[]{:S(2)}, u32[]{:S(2)}) async-start(bf16[32,8,8,128]{3,2,1,0:T(8,128)(2,1)} %get-tuple-element.17), calls=%async_computation | async-start | bytes 1048576 | tf_op jit(solution)/shard_map/all_to_all | solution.py:427
  30.8 1.2 fusion.9
  32.0 4.3 %collective-permute-start.2 = (bf16[2,3,256,128]{3,2,1,0:T(8,128)(2,1)S(1)}, bf16[2,3,256,128]{3,2,1,0:T(8,128)(2,1)S(1)}, u32[]{:S(2)}, u32[]{:S(2)}) collective-permute-start(bf16[2,3,256,128]{3,2,1,0:T(8,128)(2,1)S(1)} %get-tuple-element.27), channel_id=1, source_target_pairs={{0,30},{2,0},{4,2},{6,4},{8,6},{10,8},{12,10},{14,12},{16,14},{18,... | collective-permute-start | bytes 1179656 | tf_op jit(solution)/shard_map/ppermute | solution.py:45
  36.4 1.3 %add_divide_fusion.kernel = f32[8,256,128]{2,1,0:T(8,128)} fusion(f32[128]{0:T(128)S(1)} %fusion.8, f32[8,256]{1,0:T(8,128)S(1)} %broadcast_add_fusion), kind=kLoop, calls=%fused_computation | loop fusion | flops 786432 | bytes 1057280 | tf_op jit(solution)/shard_map/div | solution.py:424
  37.8 8.3 %all-to-all-done.spectrum = bf16[32,8,8,128]{3,2,1,0:T(8,128)(2,1)S(1)} async-done(((bf16[32,8,8,128]{3,2,1,0:T(8,128)(2,1)}), bf16[32,8,8,128]{3,2,1,0:T(8,128)(2,1)S(1)}, u32[]{:S(2)}, u32[]{:S(2)}) %all-to-all-start) | async-done | bytes 524320 | tf_op jit(solution)/shard_map/all_to_all | solution.py:427
  46.0 0.8 copy-done.1
  46.8 4.7 %filter.1 = bf16[32,8,8,128]{3,2,1,0:T(8,128)(2,1)} custom-call(bf16[32,8,8,128]{3,2,1,0:T(8,128)(2,1)} %copy-done.1, f32[8,256,128]{2,1,0:T(8,128)} %add_divide_fusion.kernel, bf16[256,256]{1,0:T(8,128)(2,1)} %constant.58.clone.refs_2_.table_x.refs_3_, bf16[256,256]{1,0:T(8,128)(2,1)} %constant.59.clone.refs_3_.table_x_low.refs_4_), custom_call_target="tpu_custom_call" | custom-call | flops 536870912 | bytes 2097152 | tf_op jit(solution)/shard_map/filter/pallas_call | solution.py:161
  51.5 7.3 %all-to-all-start.1 = ((bf16[32,8,8,128]{3,2,1,0:T(8,128)(2,1)}), bf16[32,8,8,128]{3,2,1,0:T(8,128)(2,1)S(1)}, u32[]{:S(2)}, u32[]{:S(2)}) async-start(bf16[32,8,8,128]{3,2,1,0:T(8,128)(2,1)} %filter.1), calls=%async_computation.1 | async-start | bytes 1048576 | tf_op jit(solution)/shard_map/all_to_all | solution.py:435
  58.8 1.8 %collective-permute-start.4 = (bf16[8,256,128]{2,1,0:T(8,128)(2,1)S(1)}, bf16[8,256,128]{2,1,0:T(8,128)(2,1)S(1)}, u32[]{:S(2)}, u32[]{:S(2)}) collective-permute-start(bf16[8,256,128]{2,1,0:T(8,128)(2,1)S(1)} %copy-done.8), channel_id=1, source_target_pairs={{0,1},{1,0},{2,3},{3,2},{4,5},{5,4},{6,7},{7,6},{8,9},{9,8},{10,11... | collective-permute-start | bytes 1572872 | tf_op jit(solution)/shard_map/ppermute | solution.py:45
  61.4 0.8 copy-done.6
  62.3 19.5 %stencil.1 = (f32[2,16,256,128]{3,2,1,0:T(8,128)}, f32[4,8,128]{2,1,0:T(8,128)}, bf16[8,256,128]{2,1,0:T(8,128)(2,1)}, bf16[8,256,128]{2,1,0:T(8,128)(2,1)}) custom-call(s32[1]{0:T(128)} %bitcast.turn, f32[2]{0:T(128)} %energies.1, f32[1]{0:T(128)S(6)} %copy.23.beta, bf16[2,3,256,128]{3,2,1,0:T(8,128)(2,1)} %copy-done.7, bf16[2,16,256,128]{3,2,1,0:T(8,128)(2,1)} %current.7, ...), custom_call_target="tpu_custom_call" | custom-call | flops 1610612736 | bytes 14680064 | tf_op jit(solution)/shard_map/stencil/pallas_call | solution.py:372
  82.1 13.6 %collective-permute-done.3.refs_7_ = bf16[8,256,128]{2,1,0:T(8,128)(2,1)S(1)} collective-permute-done((bf16[8,256,128]{2,1,0:T(8,128)(2,1)}, bf16[8,256,128]{2,1,0:T(8,128)(2,1)S(1)}, u32[]{:S(2)}, u32[]{:S(2)}) %collective-permute-start.3) | collective-permute-done | bytes 524320 | tf_op jit(solution)/shard_map/ppermute | solution.py:45
  95.7 0.8 copy-done.3
  96.7 4.9 %inverse.1 = (bf16[8,256,128]{2,1,0:T(8,128)(2,1)}, f32[32,8,128]{2,1,0:T(8,128)}) custom-call(bf16[32,8,8,128]{3,2,1,0:T(8,128)(2,1)} %copy-done, f32[8,256,128]{2,1,0:T(8,128)} %get-tuple-element.18.refs_1_, f32[4,8,128]{2,1,0:T(8,128)} %get-tuple-element.19.refs_2_, bf16[256,256]{1,0:T(8,128)(2,1)} %constant.58.clone.refs_2_.table_x.refs_3_, ...), custom_call_target="tpu_custom_call" | custom-call | flops 402653184 | bytes 4194304 | tf_op jit(solution)/shard_map/inverse/pallas_call | solution.py:204
  101.6 0.4 collective-permute-start.5
  102.0 14.4 %all_to_all.15.moments = f32[32,8,128]{2,1,0:T(8,128)} all-to-all(f32[32,8,128]{2,1,0:T(8,128)} %get-tuple-element.24), channel_id=1, replica_groups=mesh['dom'=16,'orb'=2] {'dom','orb'}, dimensions={0} | all-to-all | bytes 262144 | tf_op jit(solution)/shard_map/all_to_all | solution.py:440
  116.4 0.8 copy-done.4
  117.2 11.3 %final.1 = (bf16[2,16,256,128]{3,2,1,0:T(8,128)(2,1)}, f32[1]{0:T(128)}, f32[1]{0:T(128)}) custom-call(s32[1]{0:T(128)} %bitcast.turn, f32[32,8,128]{2,1,0:T(8,128)} %all_to_all.15.moments, f32[2,16,256,128]{3,2,1,0:T(8,128)} %get-tuple-element.25.fixed, bf16[2,16,256,128]{3,2,1,0:T(8,128)(2,1)} %orbitals.7, bf16[2,16,256,128]{3,2,1,0:T(8,128)(2,1)} %current.7, ...), custom_call_target="tpu_custom_call" | custom-call | flops 5242880 | bytes 11534336 | tf_op jit(solution)/shard_map/final/pallas_call | solution.py:264
  (24 shorter events, 0.7 us)
Async XLA Ops:
  4.3 15.1 %collective-permute-start = (bf16[8,256,128]{2,1,0:T(8,128)(2,1)}, bf16[8,256,128]{2,1,0:T(8,128)(2,1)S(1)}, u32[]{:S(2)}, u32[]{:S(2)}) collective-permute-start(bf16[8,256,128]{2,1,0:T(8,128)(2,1)} %get-tuple-element.16), channel_id=1, source_target_pairs={{0,1},{1,0},{2,3},{3,2},{4,5},{5,4},{6,7},{7,6},{8,9},{9,8},{10,11... | collective-permute-start | bytes 1572872 | tf_op jit(solution)/shard_map/ppermute | solution.py:45
  19.4 0.8 copy-start.5
  24.8 21.3 %all-to-all-start = ((bf16[32,8,8,128]{3,2,1,0:T(8,128)(2,1)}), bf16[32,8,8,128]{3,2,1,0:T(8,128)(2,1)S(1)}, u32[]{:S(2)}, u32[]{:S(2)}) async-start(bf16[32,8,8,128]{3,2,1,0:T(8,128)(2,1)} %get-tuple-element.17), calls=%async_computation | async-start | bytes 1048576 | tf_op jit(solution)/shard_map/all_to_all | solution.py:427
  32.0 29.3 %collective-permute-start.2 = (bf16[2,3,256,128]{3,2,1,0:T(8,128)(2,1)S(1)}, bf16[2,3,256,128]{3,2,1,0:T(8,128)(2,1)S(1)}, u32[]{:S(2)}, u32[]{:S(2)}) collective-permute-start(bf16[2,3,256,128]{3,2,1,0:T(8,128)(2,1)S(1)} %get-tuple-element.27), channel_id=1, source_target_pairs={{0,30},{2,0},{4,2},{6,4},{8,6},{10,8},{12,10},{14,12},{16,14},{18,... | collective-permute-start | bytes 1179656 | tf_op jit(solution)/shard_map/ppermute | solution.py:45
  36.3 25.0 %collective-permute-start.1 = (bf16[2,3,256,128]{3,2,1,0:T(8,128)(2,1)S(1)}, bf16[2,3,256,128]{3,2,1,0:T(8,128)(2,1)S(1)}, u32[]{:S(2)}, u32[]{:S(2)}) collective-permute-start(bf16[2,3,256,128]{3,2,1,0:T(8,128)(2,1)S(1)} %get-tuple-element.28), channel_id=1, source_target_pairs={{0,2},{2,4},{4,6},{6,8},{8,10},{10,12},{12,14},{14,16},{16,18},{18... | collective-permute-start | bytes 1179656 | tf_op jit(solution)/shard_map/ppermute | solution.py:45
  36.4 22.4 %copy-start.8 = (bf16[8,256,128]{2,1,0:T(8,128)(2,1)S(1)}, bf16[8,256,128]{2,1,0:T(8,128)(2,1)}, u32[]{:S(2)}) copy-start(bf16[8,256,128]{2,1,0:T(8,128)(2,1)} %get-tuple-element.23) | copy-start | bytes 1572868
  46.0 0.8 copy-start.1
  51.5 44.2 %all-to-all-start.1 = ((bf16[32,8,8,128]{3,2,1,0:T(8,128)(2,1)}), bf16[32,8,8,128]{3,2,1,0:T(8,128)(2,1)S(1)}, u32[]{:S(2)}, u32[]{:S(2)}) async-start(bf16[32,8,8,128]{3,2,1,0:T(8,128)(2,1)} %filter.1), calls=%async_computation.1 | async-start | bytes 1048576 | tf_op jit(solution)/shard_map/all_to_all | solution.py:435
  58.8 23.3 %collective-permute-start.4 = (bf16[8,256,128]{2,1,0:T(8,128)(2,1)S(1)}, bf16[8,256,128]{2,1,0:T(8,128)(2,1)S(1)}, u32[]{:S(2)}, u32[]{:S(2)}) collective-permute-start(bf16[8,256,128]{2,1,0:T(8,128)(2,1)S(1)} %copy-done.8), channel_id=1, source_target_pairs={{0,1},{1,0},{2,3},{3,2},{4,5},{5,4},{6,7},{7,6},{8,9},{9,8},{10,11... | collective-permute-start | bytes 1572872 | tf_op jit(solution)/shard_map/ppermute | solution.py:45
  61.3 0.8 copy-start.6
  61.3 0.9 copy-start.7
  81.8 13.9 %collective-permute-start.3 = (bf16[8,256,128]{2,1,0:T(8,128)(2,1)}, bf16[8,256,128]{2,1,0:T(8,128)(2,1)S(1)}, u32[]{:S(2)}, u32[]{:S(2)}) collective-permute-start(bf16[8,256,128]{2,1,0:T(8,128)(2,1)} %get-tuple-element.21), channel_id=1, source_target_pairs={{0,1},{1,0},{2,3},{3,2},{4,5},{5,4},{6,7},{7,6},{8,9},{9,8},{10,11... | collective-permute-start | bytes 1572872 | tf_op jit(solution)/shard_map/ppermute | solution.py:45
  82.1 13.6 %copy-start.2 = (bf16[8,256,128]{2,1,0:T(8,128)(2,1)}, bf16[8,256,128]{2,1,0:T(8,128)(2,1)S(1)}, u32[]{:S(2)}) copy-start(bf16[8,256,128]{2,1,0:T(8,128)(2,1)S(1)} %collective-permute-done.4.refs_9_) | copy-start | bytes 1572868
  95.7 0.8 copy-start.3
  95.7 1.0 copy-start
  101.6 14.8 %collective-permute-start.5 = (bf16[8,256,128]{2,1,0:T(8,128)(2,1)}, bf16[8,256,128]{2,1,0:T(8,128)(2,1)S(1)}, u32[]{:S(2)}, u32[]{:S(2)}) collective-permute-start(bf16[8,256,128]{2,1,0:T(8,128)(2,1)} %get-tuple-element.26.refs_1_), channel_id=1, source_target_pairs={{0,1},{1,0},{2,3},{3,2},{4,5},{5,4},{6,7},{7,6},{8,9},{9,8},{10,11... | collective-permute-start | bytes 1572872 | tf_op jit(solution)/shard_map/ppermute | solution.py:45
  116.4 0.8 copy-start.4
